TPU v7x, 32 devices: a whole 2x2x4 slice. The times are simulated.
32 devices in a mesh: tm: 4 (over x, core), rows: 8 (over z, y).
Axes of the slice: x: 2, y: 2, z: 4, core: 2. Of those that a mesh axis runs over, the one named last changes fastest.
Arguments:
- smoother_gains: bfloat16 [4, 1536, 1536], P('tm', 'rows'), may hold values from -1 to 1
- smoother_offsets: bfloat16 [4, 1536], P('tm', 'rows'), may hold values from -6 to 6
- smoother_covs: bfloat16 [4, 1536, 1536], P('tm', 'rows'), may hold values from -1 to 4, as said below
Outputs:
- smoothed_means: bfloat16 [4, 1536], P('tm', 'rows')
- smoothed_covs: bfloat16 [4, 1536, 1536], P('tm', 'rows')
Inputs may be any that keep to these rules, and one draw needn't show every extreme that they name: `smoother_covs`: each step's covariance matrix is symmetric.
All inputs are finite; a program needn't handle non-finite values.
Results may differ from a plain program's by a relative error of at most 0.025.
Values may be sent and summed in bfloat16 or wider, within the bound.
A program may use at most 64 MiB of HBM per device.

v0:
```python
import jax
import jax.numpy as jnp
from jax import lax
from jax.sharding import PartitionSpec as P


def from_behind(block, axis, distance):
    devices = range(lax.axis_size(axis))
    route = [(i - distance, i) for i in devices if i - distance in devices]
    return lax.ppermute(block, axis, route)


def fold_rows(left_panel, pieces):
    return tuple(
        (jnp.dot(left_panel, portion, preferred_element_type=jnp.float32) for portion in pieces)
    )


def shards(smoother_gains, smoother_offsets, smoother_covs):
    own_gain = smoother_gains[0]
    own_offset = smoother_offsets[0]
    own_cov = smoother_covs[0]
    whole_gain = lax.all_gather(own_gain, "rows", axis=0, tiled=True)
    mean_now = own_offset
    cov_now = own_cov
    for round_index in range(lax.axis_size("tm") - 1):
        mean_in, cov_in = from_behind((mean_now, cov_now), "tm", -1)
        mean_sum, left_times = fold_rows(
            own_gain,
            (
                lax.all_gather(mean_in, "rows", axis=0, tiled=True),
                lax.all_gather(cov_in, "rows", axis=0, tiled=True),
            ),
        )
        product_full = lax.dot_general(
            left_times.astype(jnp.bfloat16),
            whole_gain,
            (((1,), (1,)), ((), ())),
            preferred_element_type=jnp.float32,
        )
        mean_now = (mean_sum + own_offset.astype(jnp.float32)).astype(jnp.bfloat16)
        cov_now = (product_full + own_cov.astype(jnp.float32)).astype(jnp.bfloat16)
    return (mean_now[None], cov_now[None])


def solution(mesh):
    in_specs = (P("tm", "rows", None), P("tm", "rows"), P("tm", "rows", None))
    out_specs = (P("tm", "rows"), P("tm", "rows", None))
    return jax.shard_map(shards, mesh=mesh, in_specs=in_specs, out_specs=out_specs, check_vma=False)
```

profile of v0, /device:TPU:0, one launch (start us, length us, event | category | flops | bytes accessed | tf_op | source)
XLA Modules:
  0.0 384.1 jit_solution(2064067778634341476)
XLA Ops:
  7.2 0.7 all-gather.12.cloned.1.call-update
  7.9 1.3 collective-permute-start.3
  9.2 2.8 collective-permute-done.3
  12.1 0.8 copy-done.2
  13.0 79.8 %all-gather.12.cloned.1.call-done = bf16[1,1536,1536]{2,1,0:T(8,128)(2,1)} async-done(((bf16[1,192,1536]{2,1,0:T(8,128)(2,1)}), bf16[1,1536,1536]{2,1,0:T(8,128)(2,1)}) %all-gather.12.cloned.1.call-update) | async-done | bytes 4718608 | tf_op jit(solution)/shard_map/all_gather | solution.py:23
  92.8 80.8 %all-gather.6.cloned.1.call-done = bf16[1536,1536]{1,0:T(8,128)(2,1)} async-done(((bf16[192,1536]{1,0:T(8,128)(2,1)}), bf16[1536,1536]{1,0:T(8,128)(2,1)}) %all-gather.6.cloned.1.call-update) | async-done | bytes 4718608 | tf_op jit(solution)/shard_map/all_gather | solution.py:32
  173.6 6.6 %fusion.15 = bf16[192,1536]{1,0:T(8,128)(2,1)S(1)} fusion(bf16[1,1536,1536]{2,1,0:T(8,128)(2,1)} %all-gather.12.cloned.1.call-done, bf16[1536,1536]{1,0:T(8,128)(2,1)} %all-gather.6.cloned.1.call-done, bf16[1,192,1536]{2,1,0:T(8,128)(2,1)} %param.3, bf16[1,192,1536]{2,1,0:T(8,128)(2,1)} %param.5), kind=kOutput, calls=%fused_computation.12 | convolution fusion | flops 1813118976 | bytes 11206656 | tf_op jit(solution)/shard_map/dot_general | solution.py:35
  180.2 1.3 collective-permute-start.4
  181.5 2.6 collective-permute-done.4
  184.1 0.8 copy-done.3
  185.0 84.1 %all-gather.8.cloned.1.call-done = bf16[1536,1536]{1,0:T(8,128)(2,1)} async-done(((bf16[192,1536]{1,0:T(8,128)(2,1)}), bf16[1536,1536]{1,0:T(8,128)(2,1)}) %all-gather.8.cloned.1.call-update) | async-done | bytes 4718608 | tf_op jit(solution)/shard_map/all_gather | solution.py:32
  269.2 8.8 %fusion.21 = bf16[192,1536]{1,0:T(8,128)(2,1)S(1)} fusion(bf16[1,1536,1536]{2,1,0:T(8,128)(2,1)} %all-gather.12.cloned.1.call-done, bf16[1536,1536]{1,0:T(8,128)(2,1)} %all-gather.8.cloned.1.call-done, bf16[1,192,1536]{2,1,0:T(8,128)(2,1)S(1)} %copy-done, bf16[1,192,1536]{2,1,0:T(8,128)(2,1)S(1)} %copy-done.5), kind=kOutput, calls=%fused_computation.14 | convolution fusion | flops 1813118976 | bytes 11206656 | tf_op jit(solution)/shard_map/dot_general | solution.py:35
  278.0 1.3 collective-permute-start.5
  279.3 2.6 collective-permute-done.5
  281.9 0.8 copy-done.1
  282.7 1.3 collective-permute-start
  284.0 0.6 dynamic-slice
  285.3 7.1 %collective-permute-done = bf16[192]{0:T(256)(128)(2,1)S(1)} collective-permute-done((bf16[192]{0:T(256)(128)(2,1)S(1)}, bf16[192]{0:T(256)(128)(2,1)S(1)}, u32[]{:S(2)}, u32[]{:S(2)}) %collective-permute-start) | collective-permute-done | bytes 416 | tf_op jit(solution)/shard_map/ppermute | solution.py:10
  292.4 0.2 dynamic-update-slice
  292.6 19.1 %all-reduce = bf16[1536]{0:T(1024)(128)(2,1)S(1)} all-reduce(bf16[1536]{0:T(1024)(128)(2,1)S(1)} %dynamic-update-slice), channel_id=1, replica_groups=mesh['tm'=4,'rows'=8] {'rows'}, use_global_device_ids=true, to_apply=%add | all-reduce | flops 1536 | bytes 6144
  311.7 0.2 fusion.37
  312.0 1.3 collective-permute-start.1
  313.3 1.7 collective-permute-done.1
  315.2 17.7 %all-reduce.1 = bf16[1536]{0:T(1024)(128)(2,1)S(1)} all-reduce(bf16[1536]{0:T(1024)(128)(2,1)S(1)} %dynamic-update-slice.1), channel_id=1, replica_groups=mesh['tm'=4,'rows'=8] {'rows'}, use_global_device_ids=true, to_apply=%add.1 | all-reduce | flops 1536 | bytes 6144
  332.9 0.2 fusion.35
  333.1 1.3 collective-permute-start.2
  334.5 1.7 collective-permute-done.2
  336.4 19.7 %all-reduce.2 = bf16[1536]{0:T(1024)(128)(2,1)S(1)} all-reduce(bf16[1536]{0:T(1024)(128)(2,1)S(1)} %dynamic-update-slice.2), channel_id=1, replica_groups=mesh['tm'=4,'rows'=8] {'rows'}, use_global_device_ids=true, to_apply=%add.2 | all-reduce | flops 1536 | bytes 6144
  356.1 0.2 fusion.33
  356.4 0.6 broadcast_in_dim.6
  357.0 11.0 %all-gather.10.cloned.1.call-done = bf16[1536,1536]{1,0:T(8,128)(2,1)} async-done(((bf16[192,1536]{1,0:T(8,128)(2,1)}), bf16[1536,1536]{1,0:T(8,128)(2,1)}) %all-gather.10.cloned.1.call-update) | async-done | bytes 4718608 | tf_op jit(solution)/shard_map/all_gather | solution.py:32
  368.0 9.6 %fusion.24 = bf16[1,192,1536]{2,1,0:T(8,128)(2,1)} fusion(bf16[1,1536,1536]{2,1,0:T(8,128)(2,1)} %all-gather.12.cloned.1.call-done, bf16[1536,1536]{1,0:T(8,128)(2,1)} %all-gather.10.cloned.1.call-done, bf16[1,192,1536]{2,1,0:T(8,128)(2,1)S(1)} %copy-done, bf16[1,192,1536]{2,1,0:T(8,128)(2,1)S(1)} %copy-done.5), kind=kOutput, calls=%fused_computation.15 | convolution fusion | flops 1813118976 | bytes 11206656 | tf_op jit(solution)/shard_map/dot_general | solution.py:35
  (30 shorter events, 0.7 us)
Async XLA Ops:
  7.2 85.6 %all-gather.12.cloned.1.call-start = ((), (), s32[]{:S(2)}) async-start(), calls=%async_computation.3 | async-start | bytes 5308416 | tf_op jit(solution)/shard_map/all_gather | solution.py:23
  7.9 165.7 %all-gather.6.cloned.1.call-start = ((), (), s32[]{:S(2)}) async-start(), calls=%async_computation | async-start | bytes 5308416 | tf_op jit(solution)/shard_map/all_gather | solution.py:32
  7.9 4.1 %collective-permute-start.3 = (bf16[192,1536]{1,0:T(8,128)(2,1)}, bf16[192,1536]{1,0:T(8,128)(2,1)S(1)}, u32[]{:S(2)}, u32[]{:S(2)}) collective-permute-start(bf16[192,1536]{1,0:T(8,128)(2,1)} %bitcast.56), channel_id=1, source_target_pairs={{8,0},{16,8},{24,16},{9,1},{17,9},{25,17},{10,2},{18,10},{26,18},{... | collective-permute-start | bytes 1769480 | tf_op jit(solution)/shard_map/ppermute | solution.py:10
  12.1 0.8 copy-start.2
  12.9 256.3 %copy-start = (bf16[1,192,1536]{2,1,0:T(8,128)(2,1)S(1)}, bf16[1,192,1536]{2,1,0:T(8,128)(2,1)}, u32[]{:S(2)}) copy-start(bf16[1,192,1536]{2,1,0:T(8,128)(2,1)} %param.3) | copy-start | bytes 1769476
  12.9 256.3 %copy-start.5 = (bf16[1,192,1536]{2,1,0:T(8,128)(2,1)S(1)}, bf16[1,192,1536]{2,1,0:T(8,128)(2,1)}, u32[]{:S(2)}) copy-start(bf16[1,192,1536]{2,1,0:T(8,128)(2,1)} %param.5) | copy-start | bytes 1769476
  12.9 256.3 %all-gather.8.cloned.1.call-start = ((), (), s32[]{:S(2)}) async-start(), calls=%async_computation.1 | async-start | bytes 5308416 | tf_op jit(solution)/shard_map/all_gather | solution.py:32
  180.2 3.9 %collective-permute-start.4 = (bf16[192,1536]{1,0:T(8,128)(2,1)S(1)}, bf16[192,1536]{1,0:T(8,128)(2,1)S(1)}, u32[]{:S(2)}, u32[]{:S(2)}) collective-permute-start(bf16[192,1536]{1,0:T(8,128)(2,1)S(1)} %fusion.15), channel_id=1, source_target_pairs={{8,0},{16,8},{24,16},{9,1},{17,9},{25,17},{10,2},{18,10},{26,18},{... | collective-permute-start | bytes 1769480 | tf_op jit(solution)/shard_map/ppermute | solution.py:10
  184.1 0.8 copy-start.3
  185.0 97.7 %copy-start.4 = (bf16[1,192]{1,0:T(2,128)(2,1)S(1)}, bf16[1,192]{1,0:T(2,128)(2,1)}, u32[]{:S(2)}) copy-start(bf16[1,192]{1,0:T(2,128)(2,1)} %param.4) | copy-start | bytes 1156
  185.0 99.1 %copy-start.6 = (u32[32]{0:T(128)S(1)}, u32[32]{0:T(128)}, u32[]{:S(2)}) copy-start(u32[32]{0:T(128)} %constant.5) | copy-start | bytes 388
  185.0 183.0 %all-gather.10.cloned.1.call-start = ((), (), s32[]{:S(2)}) async-start(), calls=%async_computation.2 | async-start | bytes 5308416 | tf_op jit(solution)/shard_map/all_gather | solution.py:32
  278.0 3.9 %collective-permute-start.5 = (bf16[192,1536]{1,0:T(8,128)(2,1)S(1)}, bf16[192,1536]{1,0:T(8,128)(2,1)S(1)}, u32[]{:S(2)}, u32[]{:S(2)}) collective-permute-start(bf16[192,1536]{1,0:T(8,128)(2,1)S(1)} %fusion.21), channel_id=1, source_target_pairs={{8,0},{16,8},{24,16},{9,1},{17,9},{25,17},{10,2},{18,10},{26,18},{... | collective-permute-start | bytes 1769480 | tf_op jit(solution)/shard_map/ppermute | solution.py:10
  281.9 0.8 copy-start.1
  282.7 9.7 %collective-permute-start = (bf16[192]{0:T(256)(128)(2,1)S(1)}, bf16[192]{0:T(256)(128)(2,1)S(1)}, u32[]{:S(2)}, u32[]{:S(2)}) collective-permute-start(bf16[192]{0:T(256)(128)(2,1)S(1)} %reduce), channel_id=1, source_target_pairs={{8,0},{16,8},{24,16},{9,1},{17,9},{25,17},{10,2},{18,10},{26,18},{... | collective-permute-start | bytes 1160 | tf_op jit(solution)/shard_map/ppermute | solution.py:10
  312.0 3.0 collective-permute-start.1
  333.1 3.0 collective-permute-start.2
Sparse Core Ops, SparseCore 0:
  10.2 82.5 all-gather.11
  95.6 78.0 all-gather.5
  185.1 84.0 all-gather.7
  282.8 85.1 all-gather.9
where the time goes:
time: 384 us
  waiting for transfers between devices  275 us (72%)
  blocking collectives  56.6 us (15%)
  matrix products  25.7 us (7%)
  between operations  14.5 us (4%)
  starting transfers between devices  7.96 us (2%)
  local copies, waits for them, and re-layouts  4.25 us (1%)
    all_gather x3, waiting for transfers between devices, shards(): lax.all_gather(cov_in, 'rows', axis=0, tiled=True)  176 us
    all_gather x1, waiting for transfers between devices, shards(): whole_gain = lax.all_gather(own_gain, 'rows', axis=0, tiled=True)  79.8 us
    unnamed x3, blocking collectives  56.6 us
    dot_general x3, matrix products, shards(): lax.dot_general(left_times.astype(jnp.bfloat16), whole_gain, (((1,), (1,)...  25 us
    ppermute x6, waiting for transfers between devices, from_behind(): return lax.ppermute(block, axis, route)  18.6 us
    ppermute x6, starting transfers between devices, from_behind(): return lax.ppermute(block, axis, route)  7.8 us
  transfers between devices with their start and end apart: 10, of which 10 were waited for; matrix products, arithmetic and copies ran while one was open for 1% of the time, Pallas kernels for 0%

commit v1 on v0

--- a/solution.py
+++ b/solution.py
@@ -2,6 +2,19 @@
 import jax.numpy as jnp
 from jax import lax
 from jax.sharding import PartitionSpec as P
+
+
+def ring_gather(value, axis, dim):
+    ways = lax.axis_size(axis)
+    up = [(d, (d + 1) % ways) for d in range(ways)]
+    down = [(d, (d - 1) % ways) for d in range(ways)]
+    earlier, later = ([value], [value])
+    for _ in range(ways // 2):
+        earlier.append(lax.ppermute(earlier[-1], axis, up))
+    for _ in range((ways - 1) // 2):
+        later.append(lax.ppermute(later[-1], axis, down))
+    line = jnp.concatenate([*earlier[::-1], *later[1:]], axis=dim)
+    return jnp.roll(line, (lax.axis_index(axis) - ways // 2) * value.shape[dim], axis=dim)
 
 
 def from_behind(block, axis, distance):
@@ -27,10 +40,7 @@
         mean_in, cov_in = from_behind((mean_now, cov_now), "tm", -1)
         mean_sum, left_times = fold_rows(
             own_gain,
-            (
-                lax.all_gather(mean_in, "rows", axis=0, tiled=True),
-                lax.all_gather(cov_in, "rows", axis=0, tiled=True),
-            ),
+            (lax.all_gather(mean_in, "rows", axis=0, tiled=True), ring_gather(cov_in, "rows", 0)),
         )
         product_full = lax.dot_general(
             left_times.astype(jnp.bfloat16),

time: 384 us -> 444 us (1.16)
  starting transfers between devices: 7.96 us -> 59.4 us
  waiting for transfers between devices: 275 us -> 233 us
  local copies, waits for them, and re-layouts: 4.25 us -> 27 us
  blocking collectives: 56.6 us -> 77.6 us
  matrix products: 25.7 us -> 31.4 us
    all_gather x3 -> x0, waiting for transfers between devices: 176 us -> none  [shards(): lax.all_gather(cov_in, 'rows', axis=0, tiled=True)]
    ppermute x0 -> x21, waiting for transfers between devices: none -> 176 us  [the longest x12 127 us: ring_gather(): earlier.append(lax.ppermute(earlier[-1], axis, up))]
    all_gather x1, waiting for transfers between devices: 79.8 us -> 17.3 us  [shards(): whole_gain = lax.all_gather(own_gain, 'rows', axis=0, tiled=True)]
    ppermute x0 -> x21, starting transfers between devices: none -> 51.4 us  [the longest x9 32.8 us: ring_gather(): later.append(lax.ppermute(later[-1], axis, down))]
    unnamed x3, blocking collectives: 56.6 us -> 77.6 us
    ppermute x6, waiting for transfers between devices: 18.6 us -> 39.2 us  [from_behind(): return lax.ppermute(block, axis, route)]
    unnamed x24 -> x39, local copies, waits for them, and re-layouts: 3.64 us -> 23.8 us
    dot_general x3, matrix products: 25 us -> 30.7 us  [shards(): lax.dot_general(left_times.astype(jnp.bfloat16), whole_gain, (((1,), (1,)...]
  transfers between devices with their start and end apart: 10 -> 28, of which waited for: 10 -> 18; matrix products, arithmetic and copies ran while one was open for 1% -> 6% of each run, Pallas kernels for 0% -> 0%
where the time goes in v1:
time: 444 us; the launch traced here: 443 us
  waiting for transfers between devices  233 us (52%)
  blocking collectives  77.6 us (17%)
  starting transfers between devices  59.4 us (13%)
  matrix products  31.4 us (7%)
  local copies, waits for them, and re-layouts  27 us (6%)
  between operations  14.8 us (3%)
    ppermute x12, waiting for transfers between devices, ring_gather(): earlier.append(lax.ppermute(earlier[-1], axis, up))  127 us
    unnamed x3, blocking collectives  77.6 us
    ppermute x9, waiting for transfers between devices, ring_gather(): later.append(lax.ppermute(later[-1], axis, down))  48.6 us
    ppermute x6, waiting for transfers between devices, from_behind(): return lax.ppermute(block, axis, route)  39.2 us
    ppermute x9, starting transfers between devices, ring_gather(): later.append(lax.ppermute(later[-1], axis, down))  32.8 us
    dot_general x3, matrix products, shards(): lax.dot_general(left_times.astype(jnp.bfloat16), whole_gain, (((1,), (1,)...  30.7 us
    unnamed x39, local copies, waits for them, and re-layouts  23.8 us
    ppermute x12, starting transfers between devices, ring_gather(): earlier.append(lax.ppermute(earlier[-1], axis, up))  18.6 us
  transfers between devices with their start and end apart: 28, of which 18 were waited for; matrix products, arithmetic and copies ran while one was open for 6% of the time, Pallas kernels for 0%

profile of v1, /device:TPU:0, one launch (start us, length us, event | category | flops | bytes accessed | tf_op | source)
XLA Modules:
  0.0 443.3 jit_solution(7127490120876023505)
XLA Ops:
  9.2 2.8 collective-permute-done.3
  12.0 3.0 collective-permute-start.4
  15.0 11.1 %collective-permute-done.4 = bf16[192,1536]{1,0:T(8,128)(2,1)S(1)} collective-permute-done((bf16[192,1536]{1,0:T(8,128)(2,1)S(1)}, bf16[192,1536]{1,0:T(8,128)(2,1)S(1)}, u32[]{:S(2)}, u32[]{:S(2)}) %collective-permute-start.4) | collective-permute-done | bytes 589856 | tf_op jit(solution)/shard_map/ppermute | solution.py:13
  26.9 3.8 collective-permute-start.8
  30.8 25.0 %collective-permute-done.5 = bf16[192,1536]{1,0:T(8,128)(2,1)S(1)} collective-permute-done((bf16[192,1536]{1,0:T(8,128)(2,1)S(1)}, bf16[192,1536]{1,0:T(8,128)(2,1)S(1)}, u32[]{:S(2)}, u32[]{:S(2)}) %collective-permute-start.5) | collective-permute-done | bytes 589856 | tf_op jit(solution)/shard_map/ppermute | solution.py:13
  55.7 4.7 %collective-permute-start.9 = (bf16[192,1536]{1,0:T(8,128)(2,1)S(1)}, bf16[192,1536]{1,0:T(8,128)(2,1)S(1)}, u32[]{:S(2)}, u32[]{:S(2)}) collective-permute-start(bf16[192,1536]{1,0:T(8,128)(2,1)S(1)} %collective-permute-done.8), channel_id=1, source_target_pairs={{0,7},{1,0},{2,1},{3,2},{4,3},{5,4},{6,5},{7,6},{8,15},{9,8},{10,9... | collective-permute-start | bytes 1769480 | tf_op jit(solution)/shard_map/ppermute | solution.py:15
  60.5 30.8 %collective-permute-done.6 = bf16[192,1536]{1,0:T(8,128)(2,1)} collective-permute-done((bf16[192,1536]{1,0:T(8,128)(2,1)S(1)}, bf16[192,1536]{1,0:T(8,128)(2,1)}, u32[]{:S(2)}, u32[]{:S(2)}) %collective-permute-start.6) | collective-permute-done | bytes 589856 | tf_op jit(solution)/shard_map/ppermute | solution.py:13
  91.3 2.6 collective-permute-start.7
  93.8 17.1 %collective-permute-start.10 = (bf16[192,1536]{1,0:T(8,128)(2,1)S(1)}, bf16[192,1536]{1,0:T(8,128)(2,1)S(1)}, u32[]{:S(2)}, u32[]{:S(2)}) collective-permute-start(bf16[192,1536]{1,0:T(8,128)(2,1)S(1)} %collective-permute-done.9), channel_id=1, source_target_pairs={{0,7},{1,0},{2,1},{3,2},{4,3},{5,4},{6,5},{7,6},{8,15},{9,8},{10,9... | collective-permute-start | bytes 1769480 | tf_op jit(solution)/shard_map/ppermute | solution.py:15
  110.9 18.3 %collective-permute-done.7 = bf16[192,1536]{1,0:T(8,128)(2,1)} collective-permute-done((bf16[192,1536]{1,0:T(8,128)(2,1)}, bf16[192,1536]{1,0:T(8,128)(2,1)}, u32[]{:S(2)}, u32[]{:S(2)}) %collective-permute-start.7) | collective-permute-done | bytes 589856 | tf_op jit(solution)/shard_map/ppermute | solution.py:13
  138.4 17.3 %all-gather.3.cloned.1.call-done = bf16[1,1536,1536]{2,1,0:T(8,128)(2,1)} async-done(((bf16[1,192,1536]{2,1,0:T(8,128)(2,1)}), bf16[1,1536,1536]{2,1,0:T(8,128)(2,1)}) %all-gather.3.cloned.1.call-update) | async-done | bytes 4718608 | tf_op jit(solution)/shard_map/all_gather | solution.py:36
  155.7 10.0 %fusion.39 = bf16[192,1536]{1,0:T(8,128)(2,1)S(1)} fusion(bf16[1,1536,1536]{2,1,0:T(8,128)(2,1)} %all-gather.3.cloned.1.call-done, s32[]{:T(128)S(6)} %select_n.15, bf16[1536,1536]{1,0:T(8,128)(2,1)} %constant_dynamic-update-slice_fusion, bf16[1,192,1536]{2,1,0:T(8,128)(2,1)S(1)} %copy-done, bf16[1,192,1536]{2,1,0:T(8,128)(2,1)} %param.7), kind=kOutput, calls=%fused_computation.26 | convolution fusion | flops 1822556160 | bytes 11206660 | tf_op jit(solution)/shard_map/dot_general | solution.py:45
  167.1 9.2 %collective-permute-done.11 = bf16[192,1536]{1,0:T(8,128)(2,1)S(1)} collective-permute-done((bf16[192,1536]{1,0:T(8,128)(2,1)S(1)}, bf16[192,1536]{1,0:T(8,128)(2,1)S(1)}, u32[]{:S(2)}, u32[]{:S(2)}) %collective-permute-start.11) | collective-permute-done | bytes 589856 | tf_op jit(solution)/shard_map/ppermute | solution.py:23
  176.3 12.6 %collective-permute-done.12 = bf16[192,1536]{1,0:T(8,128)(2,1)S(1)} collective-permute-done((bf16[192,1536]{1,0:T(8,128)(2,1)S(1)}, bf16[192,1536]{1,0:T(8,128)(2,1)S(1)}, u32[]{:S(2)}, u32[]{:S(2)}) %collective-permute-start.12) | collective-permute-done | bytes 589856 | tf_op jit(solution)/shard_map/ppermute | solution.py:13
  188.9 4.7 %collective-permute-start.16 = (bf16[192,1536]{1,0:T(8,128)(2,1)S(1)}, bf16[192,1536]{1,0:T(8,128)(2,1)S(1)}, u32[]{:S(2)}, u32[]{:S(2)}) collective-permute-start(bf16[192,1536]{1,0:T(8,128)(2,1)S(1)} %collective-permute-done.11), channel_id=1, source_target_pairs={{0,7},{1,0},{2,1},{3,2},{4,3},{5,4},{6,5},{7,6},{8,15},{9,8},{10,9... | collective-permute-start | bytes 1769480 | tf_op jit(solution)/shard_map/ppermute | solution.py:15
  193.6 17.1 %collective-permute-done.13 = bf16[192,1536]{1,0:T(8,128)(2,1)S(1)} collective-permute-done((bf16[192,1536]{1,0:T(8,128)(2,1)S(1)}, bf16[192,1536]{1,0:T(8,128)(2,1)S(1)}, u32[]{:S(2)}, u32[]{:S(2)}) %collective-permute-start.13) | collective-permute-done | bytes 589856 | tf_op jit(solution)/shard_map/ppermute | solution.py:13
  210.7 2.6 collective-permute-start.14
  213.3 11.4 %collective-permute-done.16 = bf16[192,1536]{1,0:T(8,128)(2,1)S(1)} collective-permute-done((bf16[192,1536]{1,0:T(8,128)(2,1)S(1)}, bf16[192,1536]{1,0:T(8,128)(2,1)S(1)}, u32[]{:S(2)}, u32[]{:S(2)}) %collective-permute-start.16) | collective-permute-done | bytes 589856 | tf_op jit(solution)/shard_map/ppermute | solution.py:15
  224.8 2.1 collective-permute-start.15
  226.8 28.3 %collective-permute-done.17 = bf16[192,1536]{1,0:T(8,128)(2,1)S(1)} collective-permute-done((bf16[192,1536]{1,0:T(8,128)(2,1)S(1)}, bf16[192,1536]{1,0:T(8,128)(2,1)S(1)}, u32[]{:S(2)}, u32[]{:S(2)}) %collective-permute-start.17) | collective-permute-done | bytes 589856 | tf_op jit(solution)/shard_map/ppermute | solution.py:15
  261.3 7.4 %collective-permute-done.18 = bf16[192,1536]{1,0:T(8,128)(2,1)S(1)} collective-permute-done((bf16[192,1536]{1,0:T(8,128)(2,1)S(1)}, bf16[192,1536]{1,0:T(8,128)(2,1)S(1)}, u32[]{:S(2)}, u32[]{:S(2)}) %collective-permute-start.18) | collective-permute-done | bytes 589856 | tf_op jit(solution)/shard_map/ppermute | solution.py:15
  269.6 9.9 %fusion.36 = bf16[192,1536]{1,0:T(8,128)(2,1)S(1)} fusion(bf16[1,1536,1536]{2,1,0:T(8,128)(2,1)} %all-gather.3.cloned.1.call-done, s32[]{:T(128)S(6)} %select_n.15, bf16[1536,1536]{1,0:T(8,128)(2,1)} %constant_dynamic-update-slice_fusion.8, bf16[1,192,1536]{2,1,0:T(8,128)(2,1)S(1)} %copy-done, bf16[1,192,1536]{2,1,0:T(8,128)(2,1)S(1)} %copy-done.2), kind=kOutput, calls=%fused_computation.25 | convolution fusion | flops 1822556160 | bytes 11206660 | tf_op jit(solution)/shard_map/dot_general | solution.py:45
  280.8 5.1 %collective-permute-done.19 = bf16[192,1536]{1,0:T(8,128)(2,1)S(1)} collective-permute-done((bf16[192,1536]{1,0:T(8,128)(2,1)S(1)}, bf16[192,1536]{1,0:T(8,128)(2,1)S(1)}, u32[]{:S(2)}, u32[]{:S(2)}) %collective-permute-start.19) | collective-permute-done | bytes 589856 | tf_op jit(solution)/shard_map/ppermute | solution.py:23
  286.1 12.4 %collective-permute-done.20 = bf16[192,1536]{1,0:T(8,128)(2,1)S(1)} collective-permute-done((bf16[192,1536]{1,0:T(8,128)(2,1)S(1)}, bf16[192,1536]{1,0:T(8,128)(2,1)S(1)}, u32[]{:S(2)}, u32[]{:S(2)}) %collective-permute-start.20) | collective-permute-done | bytes 589856 | tf_op jit(solution)/shard_map/ppermute | solution.py:13
  301.1 18.7 %collective-permute-done = bf16[192]{0:T(256)(128)(2,1)S(1)} collective-permute-done((bf16[192]{0:T(256)(128)(2,1)S(1)}, bf16[192]{0:T(256)(128)(2,1)S(1)}, u32[]{:S(2)}, u32[]{:S(2)}) %collective-permute-start) | collective-permute-done | bytes 416 | tf_op jit(solution)/shard_map/ppermute | solution.py:23
  319.9 21.5 %all-reduce = bf16[1536]{0:T(1024)(128)(2,1)S(1)} all-reduce(bf16[1536]{0:T(1024)(128)(2,1)S(1)} %dynamic-update-slice), channel_id=1, replica_groups=mesh['tm'=4,'rows'=8] {'rows'}, use_global_device_ids=true, to_apply=%add | all-reduce | flops 1536 | bytes 6144
  341.6 2.0 collective-permute-start.22
  347.0 30.9 %all-reduce.1 = bf16[1536]{0:T(1024)(128)(2,1)S(1)} all-reduce(bf16[1536]{0:T(1024)(128)(2,1)S(1)} %dynamic-update-slice.1), channel_id=1, replica_groups=mesh['tm'=4,'rows'=8] {'rows'}, use_global_device_ids=true, to_apply=%add.1 | all-reduce | flops 1536 | bytes 6144
  378.2 2.0 collective-permute-start.25
  380.2 5.3 %collective-permute-start.23 = (bf16[192,1536]{1,0:T(8,128)(2,1)S(1)}, bf16[192,1536]{1,0:T(8,128)(2,1)}, u32[]{:S(2)}, u32[]{:S(2)}) collective-permute-start(bf16[192,1536]{1,0:T(8,128)(2,1)S(1)} %collective-permute-done.22), channel_id=1, source_target_pairs={{0,1},{1,2},{2,3},{3,4},{4,5},{5,6},{6,7},{7,0},{8,9},{9,10},{10,1... | collective-permute-start | bytes 1769480 | tf_op jit(solution)/shard_map/ppermute | solution.py:13
  388.7 25.2 %all-reduce.2 = bf16[1536]{0:T(1024)(128)(2,1)S(1)} all-reduce(bf16[1536]{0:T(1024)(128)(2,1)S(1)} %dynamic-update-slice.2), channel_id=1, replica_groups=mesh['tm'=4,'rows'=8] {'rows'}, use_global_device_ids=true, to_apply=%add.2 | all-reduce | flops 1536 | bytes 6144
  425.7 10.8 %fusion.42 = bf16[1,192,1536]{2,1,0:T(8,128)(2,1)} fusion(bf16[1,1536,1536]{2,1,0:T(8,128)(2,1)} %all-gather.3.cloned.1.call-done, s32[]{:T(128)S(6)} %select_n.15, bf16[1536,1536]{1,0:T(8,128)(2,1)} %constant_dynamic-update-slice_fusion.16, bf16[1,192,1536]{2,1,0:T(8,128)(2,1)S(1)} %copy-done, bf16[1,192,1536]{2,1,0:T(8,128)(2,1)} %param.7), kind=kOutput, calls=%fused_computation.27 | convolution fusion | flops 1822556160 | bytes 11206660 | tf_op jit(solution)/shard_map/dot_general | solution.py:45
  (81 shorter events, 42.9 us)
Async XLA Ops:
  7.2 148.6 %all-gather.3.cloned.1.call-start = ((), (), s32[]{:S(2)}) async-start(), calls=%async_computation | async-start | bytes 5308416 | tf_op jit(solution)/shard_map/all_gather | solution.py:36
  7.9 4.1 collective-permute-start.3
  12.0 14.0 %collective-permute-start.4 = (bf16[192,1536]{1,0:T(8,128)(2,1)S(1)}, bf16[192,1536]{1,0:T(8,128)(2,1)S(1)}, u32[]{:S(2)}, u32[]{:S(2)}) collective-permute-start(bf16[192,1536]{1,0:T(8,128)(2,1)S(1)} %collective-permute-done.3), channel_id=1, source_target_pairs={{0,1},{1,2},{2,3},{3,4},{4,5},{5,6},{6,7},{7,0},{8,9},{9,10},{10,1... | collective-permute-start | bytes 1769480 | tf_op jit(solution)/shard_map/ppermute | solution.py:13
  26.0 29.7 %collective-permute-start.5 = (bf16[192,1536]{1,0:T(8,128)(2,1)S(1)}, bf16[192,1536]{1,0:T(8,128)(2,1)S(1)}, u32[]{:S(2)}, u32[]{:S(2)}) collective-permute-start(bf16[192,1536]{1,0:T(8,128)(2,1)S(1)} %collective-permute-done.4), channel_id=1, source_target_pairs={{0,1},{1,2},{2,3},{3,4},{4,5},{5,6},{6,7},{7,0},{8,9},{9,10},{10,1... | collective-permute-start | bytes 1769480 | tf_op jit(solution)/shard_map/ppermute | solution.py:13
  26.9 28.8 %collective-permute-start.8 = (bf16[192,1536]{1,0:T(8,128)(2,1)S(1)}, bf16[192,1536]{1,0:T(8,128)(2,1)S(1)}, u32[]{:S(2)}, u32[]{:S(2)}) collective-permute-start(bf16[192,1536]{1,0:T(8,128)(2,1)S(1)} %collective-permute-done.3), channel_id=1, source_target_pairs={{0,7},{1,0},{2,1},{3,2},{4,3},{5,4},{6,5},{7,6},{8,15},{9,8},{10,9... | collective-permute-start | bytes 1769480 | tf_op jit(solution)/shard_map/ppermute | solution.py:15
  55.7 35.5 %collective-permute-start.6 = (bf16[192,1536]{1,0:T(8,128)(2,1)S(1)}, bf16[192,1536]{1,0:T(8,128)(2,1)}, u32[]{:S(2)}, u32[]{:S(2)}) collective-permute-start(bf16[192,1536]{1,0:T(8,128)(2,1)S(1)} %collective-permute-done.5), channel_id=1, source_target_pairs={{0,1},{1,2},{2,3},{3,4},{4,5},{5,6},{6,7},{7,0},{8,9},{9,10},{10,1... | collective-permute-start | bytes 1769480 | tf_op jit(solution)/shard_map/ppermute | solution.py:13
  55.7 38.1 %collective-permute-start.9 = (bf16[192,1536]{1,0:T(8,128)(2,1)S(1)}, bf16[192,1536]{1,0:T(8,128)(2,1)S(1)}, u32[]{:S(2)}, u32[]{:S(2)}) collective-permute-start(bf16[192,1536]{1,0:T(8,128)(2,1)S(1)} %collective-permute-done.8), channel_id=1, source_target_pairs={{0,7},{1,0},{2,1},{3,2},{4,3},{5,4},{6,5},{7,6},{8,15},{9,8},{10,9... | collective-permute-start | bytes 1769480 | tf_op jit(solution)/shard_map/ppermute | solution.py:15
  91.3 38.0 %collective-permute-start.7 = (bf16[192,1536]{1,0:T(8,128)(2,1)}, bf16[192,1536]{1,0:T(8,128)(2,1)}, u32[]{:S(2)}, u32[]{:S(2)}) collective-permute-start(bf16[192,1536]{1,0:T(8,128)(2,1)} %collective-permute-done.6), channel_id=1, source_target_pairs={{0,1},{1,2},{2,3},{3,4},{4,5},{5,6},{6,7},{7,0},{8,9},{9,10},{10,1... | collective-permute-start | bytes 1769480 | tf_op jit(solution)/shard_map/ppermute | solution.py:13
  93.8 61.9 %copy-start = (bf16[1,192,1536]{2,1,0:T(8,128)(2,1)S(1)}, bf16[1,192,1536]{2,1,0:T(8,128)(2,1)}, u32[]{:S(2)}) copy-start(bf16[1,192,1536]{2,1,0:T(8,128)(2,1)} %param.5) | copy-start | bytes 1769476
  93.8 43.7 %collective-permute-start.10 = (bf16[192,1536]{1,0:T(8,128)(2,1)S(1)}, bf16[192,1536]{1,0:T(8,128)(2,1)S(1)}, u32[]{:S(2)}, u32[]{:S(2)}) collective-permute-start(bf16[192,1536]{1,0:T(8,128)(2,1)S(1)} %collective-permute-done.9), channel_id=1, source_target_pairs={{0,7},{1,0},{2,1},{3,2},{4,3},{5,4},{6,5},{7,6},{8,15},{9,8},{10,9... | collective-permute-start | bytes 1769480 | tf_op jit(solution)/shard_map/ppermute | solution.py:15
  165.7 103.9 %copy-start.2 = (bf16[1,192,1536]{2,1,0:T(8,128)(2,1)S(1)}, bf16[1,192,1536]{2,1,0:T(8,128)(2,1)}, u32[]{:S(2)}) copy-start(bf16[1,192,1536]{2,1,0:T(8,128)(2,1)} %param.7) | copy-start | bytes 1769476
  165.7 10.6 %collective-permute-start.11 = (bf16[192,1536]{1,0:T(8,128)(2,1)S(1)}, bf16[192,1536]{1,0:T(8,128)(2,1)S(1)}, u32[]{:S(2)}, u32[]{:S(2)}) collective-permute-start(bf16[192,1536]{1,0:T(8,128)(2,1)S(1)} %fusion.39), channel_id=1, source_target_pairs={{8,0},{16,8},{24,16},{9,1},{17,9},{25,17},{10,2},{18,10},{26,18},{... | collective-permute-start | bytes 1769480 | tf_op jit(solution)/shard_map/ppermute | solution.py:23
  176.3 12.6 %collective-permute-start.12 = (bf16[192,1536]{1,0:T(8,128)(2,1)S(1)}, bf16[192,1536]{1,0:T(8,128)(2,1)S(1)}, u32[]{:S(2)}, u32[]{:S(2)}) collective-permute-start(bf16[192,1536]{1,0:T(8,128)(2,1)S(1)} %collective-permute-done.11), channel_id=1, source_target_pairs={{0,1},{1,2},{2,3},{3,4},{4,5},{5,6},{6,7},{7,0},{8,9},{9,10},{10,1... | collective-permute-start | bytes 1769480 | tf_op jit(solution)/shard_map/ppermute | solution.py:13
  188.9 21.8 %collective-permute-start.13 = (bf16[192,1536]{1,0:T(8,128)(2,1)S(1)}, bf16[192,1536]{1,0:T(8,128)(2,1)S(1)}, u32[]{:S(2)}, u32[]{:S(2)}) collective-permute-start(bf16[192,1536]{1,0:T(8,128)(2,1)S(1)} %collective-permute-done.12), channel_id=1, source_target_pairs={{0,1},{1,2},{2,3},{3,4},{4,5},{5,6},{6,7},{7,0},{8,9},{9,10},{10,1... | collective-permute-start | bytes 1769480 | tf_op jit(solution)/shard_map/ppermute | solution.py:13
  188.9 35.9 %collective-permute-start.16 = (bf16[192,1536]{1,0:T(8,128)(2,1)S(1)}, bf16[192,1536]{1,0:T(8,128)(2,1)S(1)}, u32[]{:S(2)}, u32[]{:S(2)}) collective-permute-start(bf16[192,1536]{1,0:T(8,128)(2,1)S(1)} %collective-permute-done.11), channel_id=1, source_target_pairs={{0,7},{1,0},{2,1},{3,2},{4,3},{5,4},{6,5},{7,6},{8,15},{9,8},{10,9... | collective-permute-start | bytes 1769480 | tf_op jit(solution)/shard_map/ppermute | solution.py:15
  210.7 14.1 %collective-permute-start.14 = (bf16[192,1536]{1,0:T(8,128)(2,1)S(1)}, bf16[192,1536]{1,0:T(8,128)(2,1)S(1)}, u32[]{:S(2)}, u32[]{:S(2)}) collective-permute-start(bf16[192,1536]{1,0:T(8,128)(2,1)S(1)} %collective-permute-done.13), channel_id=1, source_target_pairs={{0,1},{1,2},{2,3},{3,4},{4,5},{5,6},{6,7},{7,0},{8,9},{9,10},{10,1... | collective-permute-start | bytes 1769480 | tf_op jit(solution)/shard_map/ppermute | solution.py:13
  224.8 30.4 %collective-permute-start.17 = (bf16[192,1536]{1,0:T(8,128)(2,1)S(1)}, bf16[192,1536]{1,0:T(8,128)(2,1)S(1)}, u32[]{:S(2)}, u32[]{:S(2)}) collective-permute-start(bf16[192,1536]{1,0:T(8,128)(2,1)S(1)} %collective-permute-done.16), channel_id=1, source_target_pairs={{0,7},{1,0},{2,1},{3,2},{4,3},{5,4},{6,5},{7,6},{8,15},{9,8},{10,9... | collective-permute-start | bytes 1769480 | tf_op jit(solution)/shard_map/ppermute | solution.py:15
  224.8 30.4 %collective-permute-start.15 = (bf16[192,1536]{1,0:T(8,128)(2,1)S(1)}, bf16[192,1536]{1,0:T(8,128)(2,1)S(1)}, u32[]{:S(2)}, u32[]{:S(2)}) collective-permute-start(bf16[192,1536]{1,0:T(8,128)(2,1)S(1)} %collective-permute-done.14), channel_id=1, source_target_pairs={{0,1},{1,2},{2,3},{3,4},{4,5},{5,6},{6,7},{7,0},{8,9},{9,10},{10,1... | collective-permute-start | bytes 1769480 | tf_op jit(solution)/shard_map/ppermute | solution.py:13
  255.2 13.5 %collective-permute-start.18 = (bf16[192,1536]{1,0:T(8,128)(2,1)S(1)}, bf16[192,1536]{1,0:T(8,128)(2,1)S(1)}, u32[]{:S(2)}, u32[]{:S(2)}) collective-permute-start(bf16[192,1536]{1,0:T(8,128)(2,1)S(1)} %collective-permute-done.17), channel_id=1, source_target_pairs={{0,7},{1,0},{2,1},{3,2},{4,3},{5,4},{6,5},{7,6},{8,15},{9,8},{10,9... | collective-permute-start | bytes 1769480 | tf_op jit(solution)/shard_map/ppermute | solution.py:15
  269.6 28.9 %copy-start.1 = (bf16[1,192]{1,0:T(2,128)(2,1)S(1)}, bf16[1,192]{1,0:T(2,128)(2,1)}, u32[]{:S(2)}) copy-start(bf16[1,192]{1,0:T(2,128)(2,1)} %param.6) | copy-start | bytes 1156
  269.6 30.3 %copy-start.3 = (u32[32]{0:T(128)S(1)}, u32[32]{0:T(128)}, u32[]{:S(2)}) copy-start(u32[32]{0:T(128)} %constant.28) | copy-start | bytes 388
  279.5 6.4 %collective-permute-start.19 = (bf16[192,1536]{1,0:T(8,128)(2,1)S(1)}, bf16[192,1536]{1,0:T(8,128)(2,1)S(1)}, u32[]{:S(2)}, u32[]{:S(2)}) collective-permute-start(bf16[192,1536]{1,0:T(8,128)(2,1)S(1)} %fusion.36), channel_id=1, source_target_pairs={{8,0},{16,8},{24,16},{9,1},{17,9},{25,17},{10,2},{18,10},{26,18},{... | collective-permute-start | bytes 1769480 | tf_op jit(solution)/shard_map/ppermute | solution.py:23
  285.9 12.6 %collective-permute-start.20 = (bf16[192,1536]{1,0:T(8,128)(2,1)S(1)}, bf16[192,1536]{1,0:T(8,128)(2,1)S(1)}, u32[]{:S(2)}, u32[]{:S(2)}) collective-permute-start(bf16[192,1536]{1,0:T(8,128)(2,1)S(1)} %collective-permute-done.19), channel_id=1, source_target_pairs={{0,1},{1,2},{2,3},{3,4},{4,5},{5,6},{6,7},{7,0},{8,9},{9,10},{10,1... | collective-permute-start | bytes 1769480 | tf_op jit(solution)/shard_map/ppermute | solution.py:13
  298.5 43.1 %collective-permute-start.21 = (bf16[192,1536]{1,0:T(8,128)(2,1)S(1)}, bf16[192,1536]{1,0:T(8,128)(2,1)S(1)}, u32[]{:S(2)}, u32[]{:S(2)}) collective-permute-start(bf16[192,1536]{1,0:T(8,128)(2,1)S(1)} %collective-permute-done.20), channel_id=1, source_target_pairs={{0,1},{1,2},{2,3},{3,4},{4,5},{5,6},{6,7},{7,0},{8,9},{9,10},{10,1... | collective-permute-start | bytes 1769480 | tf_op jit(solution)/shard_map/ppermute | solution.py:13
  298.5 21.2 %collective-permute-start = (bf16[192]{0:T(256)(128)(2,1)S(1)}, bf16[192]{0:T(256)(128)(2,1)S(1)}, u32[]{:S(2)}, u32[]{:S(2)}) collective-permute-start(bf16[192]{0:T(256)(128)(2,1)S(1)} %reduce), channel_id=1, source_target_pairs={{8,0},{16,8},{24,16},{9,1},{17,9},{25,17},{10,2},{18,10},{26,18},{... | collective-permute-start | bytes 1160 | tf_op jit(solution)/shard_map/ppermute | solution.py:23
  341.5 36.7 %collective-permute-start.24 = (bf16[192,1536]{1,0:T(8,128)(2,1)S(1)}, bf16[192,1536]{1,0:T(8,128)(2,1)S(1)}, u32[]{:S(2)}, u32[]{:S(2)}) collective-permute-start(bf16[192,1536]{1,0:T(8,128)(2,1)S(1)} %collective-permute-done.19), channel_id=1, source_target_pairs={{0,7},{1,0},{2,1},{3,2},{4,3},{5,4},{6,5},{7,6},{8,15},{9,8},{10,9... | collective-permute-start | bytes 1769480 | tf_op jit(solution)/shard_map/ppermute | solution.py:15
  341.6 38.6 %collective-permute-start.22 = (bf16[192,1536]{1,0:T(8,128)(2,1)S(1)}, bf16[192,1536]{1,0:T(8,128)(2,1)S(1)}, u32[]{:S(2)}, u32[]{:S(2)}) collective-permute-start(bf16[192,1536]{1,0:T(8,128)(2,1)S(1)} %collective-permute-done.21), channel_id=1, source_target_pairs={{0,1},{1,2},{2,3},{3,4},{4,5},{5,6},{6,7},{7,0},{8,9},{9,10},{10,1... | collective-permute-start | bytes 1769480 | tf_op jit(solution)/shard_map/ppermute | solution.py:13
  343.8 3.0 collective-permute-start.1
  378.2 36.5 %collective-permute-start.25 = (bf16[192,1536]{1,0:T(8,128)(2,1)S(1)}, bf16[192,1536]{1,0:T(8,128)(2,1)}, u32[]{:S(2)}, u32[]{:S(2)}) collective-permute-start(bf16[192,1536]{1,0:T(8,128)(2,1)S(1)} %collective-permute-done.24), channel_id=1, source_target_pairs={{0,7},{1,0},{2,1},{3,2},{4,3},{5,4},{6,5},{7,6},{8,15},{9,8},{10,9... | collective-permute-start | bytes 1769480 | tf_op jit(solution)/shard_map/ppermute | solution.py:15
  380.2 34.9 %collective-permute-start.23 = (bf16[192,1536]{1,0:T(8,128)(2,1)S(1)}, bf16[192,1536]{1,0:T(8,128)(2,1)}, u32[]{:S(2)}, u32[]{:S(2)}) collective-permute-start(bf16[192,1536]{1,0:T(8,128)(2,1)S(1)} %collective-permute-done.22), channel_id=1, source_target_pairs={{0,1},{1,2},{2,3},{3,4},{4,5},{5,6},{6,7},{7,0},{8,9},{9,10},{10,1... | collective-permute-start | bytes 1769480 | tf_op jit(solution)/shard_map/ppermute | solution.py:13
  385.5 3.0 collective-permute-start.2
  414.7 10.1 %collective-permute-start.26 = (bf16[192,1536]{1,0:T(8,128)(2,1)}, bf16[192,1536]{1,0:T(8,128)(2,1)S(1)}, u32[]{:S(2)}, u32[]{:S(2)}) collective-permute-start(bf16[192,1536]{1,0:T(8,128)(2,1)} %collective-permute-done.25), channel_id=1, source_target_pairs={{0,7},{1,0},{2,1},{3,2},{4,3},{5,4},{6,5},{7,6},{8,15},{9,8},{10,9... | collective-permute-start | bytes 1769480 | tf_op jit(solution)/shard_map/ppermute | solution.py:15
Sparse Core Ops, SparseCore 0:
  10.2 145.4 all-gather.2
